TPU v7x, 32 devices: a whole 2x2x4 slice. The times are simulated.
32 devices in a mesh: grp: 2 (over y), dev: 16 (over z, x, core).
Axes of the slice: x: 2, y: 2, z: 4, core: 2. Of those that a mesh axis runs over, the one named last changes fastest.
Arguments:
- spectra: float32 [256, 2, 2, 4096], P(('grp', 'dev')), may hold values from -100 to 100
- source_pick: int32 [32], P(('grp', 'dev')), may hold values from 0 to 7
- pair_remote: int32 [2, 16, 2, 2], P('grp', 'dev'), may hold values from 0 to 7
- pair_local: int32 [2, 16, 2, 2], P('grp', 'dev'), may hold values from 0 to 7
- pair_count: int32 [2, 16, 2], P('grp', 'dev'), may hold values from 0 to 2, as said below
Outputs:
- group_corr: float32 [256, 16, 512], P(('grp', 'dev'))
- cross_corr: float32 [2, 16, 2, 2, 512], P('grp', 'dev')
Inputs may be any that keep to these rules, and one draw needn't show every extreme that they name: `pair_count`: A block has no pairs with its own group and at most 2 with any other; in every group some block has exactly 2 with some other group.
All inputs are finite; a program needn't handle non-finite values.
Results may differ from a plain program's by a relative error of at most 0.0075.
Values may be sent and summed in bfloat16 or wider, within the bound.
A program may use at most 64 MiB of HBM per device.

v0:
```python
import math
import jax
import jax.numpy as jnp
from jax import lax
from jax.sharding import PartitionSpec as P

F = 4096
LAGS = 512
LAG_BLK = 128
BAND = 64
source_block = 16


def whiten(spectra):
    magnitude = jnp.sqrt(spectra[:, :, 0] * spectra[:, :, 0] + spectra[:, :, 1] * spectra[:, :, 1])
    rows_here, segments, bins = magnitude.shape
    band_mean = jnp.mean(magnitude.reshape(rows_here, segments, bins // BAND, BAND), axis=3) + 1e-05
    divisor = jnp.repeat(band_mean, BAND, axis=2)
    return (spectra / divisor[:, :, None, :]).astype(jnp.bfloat16)


def lag_tables():
    frequency = jnp.arange(F, dtype=jnp.int32)
    lag_index = jnp.arange(LAG_BLK, dtype=jnp.int32)
    phase_index = frequency[:, None] * lag_index[None, :] % (2 * F)
    angles = phase_index.astype(jnp.float32) * (math.pi / F)
    return (jnp.cos(angles).astype(jnp.bfloat16), (-jnp.sin(angles)).astype(jnp.bfloat16))


def lag_turn(block_index):
    frequency = jnp.arange(F, dtype=jnp.int32)
    phase_index = frequency * (LAG_BLK * block_index - LAGS // 2) % (2 * F)
    angles = phase_index.astype(jnp.float32) * (math.pi / F)
    return (jnp.cos(angles), jnp.sin(angles))


def cross_to_lags(cross_real, cross_imag, tables):
    cos_table, sin_table = tables
    lag_blocks = []
    for block_index in range(LAGS // LAG_BLK):
        turn_cos, turn_sin = lag_turn(block_index)
        rot_real = (cross_real * turn_cos - cross_imag * turn_sin).astype(jnp.bfloat16)
        rot_imag = (cross_real * turn_sin + cross_imag * turn_cos).astype(jnp.bfloat16)
        lag_blocks.append(
            jnp.dot(rot_real, cos_table, preferred_element_type=jnp.float32)
            + jnp.dot(rot_imag, sin_table, preferred_element_type=jnp.float32)
        )
    return jnp.concatenate(lag_blocks, axis=1) * F ** (-0.5)


def outer_cross(left_rows, right_rows):
    left_float = left_rows.astype(jnp.float32)
    right_float = right_rows.astype(jnp.float32)
    segments = left_rows.shape[1]
    cross_real = jnp.zeros((left_rows.shape[0], right_rows.shape[0], F), jnp.float32)
    cross_imag = jnp.zeros((left_rows.shape[0], right_rows.shape[0], F), jnp.float32)
    for segment in range(segments):
        left_real = left_float[:, segment, 0][:, None]
        left_imag = left_float[:, segment, 1][:, None]
        right_real = right_float[:, segment, 0][None]
        right_imag = right_float[:, segment, 1][None]
        cross_real = cross_real + (left_real * right_real + left_imag * right_imag)
        cross_imag = cross_imag + (left_imag * right_real - left_real * right_imag)
    inverse = 1.0 / segments
    return ((cross_real * inverse).reshape(-1, F), (cross_imag * inverse).reshape(-1, F))


def pair_cross(left_rows, right_rows):
    left_float = left_rows.astype(jnp.float32)
    right_float = right_rows.astype(jnp.float32)
    segments = left_rows.shape[1]
    cross_real = jnp.zeros((left_rows.shape[0], F), jnp.float32)
    cross_imag = jnp.zeros((left_rows.shape[0], F), jnp.float32)
    for segment in range(segments):
        left_real = left_float[:, segment, 0]
        left_imag = left_float[:, segment, 1]
        right_real = right_float[:, segment, 0]
        right_imag = right_float[:, segment, 1]
        cross_real = cross_real + (left_real * right_real + left_imag * right_imag)
        cross_imag = cross_imag + (left_imag * right_real - left_real * right_imag)
    inverse = 1.0 / segments
    return (cross_real * inverse, cross_imag * inverse)


def outer_lags(left_rows, right_rows, tables):
    cross_real, cross_imag = outer_cross(left_rows, right_rows)
    return cross_to_lags(cross_real, cross_imag, tables).reshape(
        left_rows.shape[0], right_rows.shape[0], LAGS
    )


def on_device(spectra, source_pick, pair_remote, pair_local, pair_count):
    white = whiten(spectra)
    channels_here = white.shape[0]
    flattened = white.reshape(channels_here, -1)
    tables = lag_tables()
    channel_ids = jnp.arange(channels_here, dtype=jnp.int32)
    picker = (channel_ids[None, :] == source_pick[:, None]).astype(jnp.bfloat16)
    source = jnp.dot(picker, flattened, preferred_element_type=jnp.float32).astype(jnp.bfloat16)
    source = source.reshape((1,) + white.shape[1:])

    def correlate(shard_rows):
        rows_here = shard_rows.shape[0]
        if rows_here > source_block and rows_here % source_block == 0:
            portions = shard_rows.reshape(
                (rows_here // source_block, source_block) + shard_rows.shape[1:]
            )
            result = lax.map(lambda portion: outer_lags(white, portion, tables), portions)
            return jnp.transpose(result, (1, 0, 2, 3)).reshape(channels_here, rows_here, LAGS)
        return outer_lags(white, shard_rows, tables)

    group_corr = correlate(lax.all_gather(source, "dev", axis=0, tiled=True))
    groups = lax.axis_size("grp")
    remote_ids = pair_remote.reshape(groups, -1)
    local_ids = pair_local.reshape(groups, -1)
    slot_count = remote_ids.shape[1]
    gathered = lax.all_gather(white[None], "grp", axis=0, tiled=True)
    remote_picker = (remote_ids[:, :, None] == channel_ids[None, None, :]).astype(jnp.bfloat16)
    remote_rows = jnp.einsum(
        "hkc,hcx->hkx",
        remote_picker,
        gathered.reshape(groups, channels_here, -1),
        preferred_element_type=jnp.float32,
    ).astype(jnp.bfloat16)
    local_picker = (local_ids.reshape(-1)[:, None] == channel_ids[None, :]).astype(jnp.bfloat16)
    local_rows = jnp.dot(local_picker, flattened, preferred_element_type=jnp.float32).astype(
        jnp.bfloat16
    )
    cross_real, cross_imag = pair_cross(
        local_rows.reshape((-1,) + white.shape[1:]), remote_rows.reshape((-1,) + white.shape[1:])
    )
    lags_out = cross_to_lags(cross_real, cross_imag, tables).reshape(groups, slot_count, LAGS)
    valid_mask = (jnp.arange(slot_count)[None, :] < pair_count.reshape(groups, 1)).astype(
        jnp.float32
    )
    cross_corr = (lags_out * valid_mask[:, :, None]).reshape(1, 1, groups, slot_count, LAGS)
    return (group_corr, cross_corr)


def solution(mesh):
    return jax.shard_map(
        on_device,
        mesh=mesh,
        in_specs=(
            P(("grp", "dev"), None, None, None),
            P(("grp", "dev")),
            P("grp", "dev", None, None),
            P("grp", "dev", None, None),
            P("grp", "dev", None),
        ),
        out_specs=(P(("grp", "dev"), None, None), P("grp", "dev", None, None, None)),
        check_vma=False,
    )
```

profile of v0, /device:TPU:0, one launch (start us, length us, event | category | flops | bytes accessed | tf_op | source)
XLA Modules:
  0.0 193.7 jit_solution(853574657091264866)
XLA Ops:
  1.3 0.8 eq.73
  2.0 0.7 compare_select_fusion
  3.0 1.4 copy.52
  6.3 24.6 %all_gather.6 = bf16[16,2,2,4096]{3,2,1,0:T(2,128)(2,1)S(1)} all-gather(bf16[1,2,2,4096]{3,2,1,0:T(2,128)(2,1)S(1)} %reshape.266), channel_id=1, replica_groups=mesh['grp'=2,'dev'=16] {'dev'}, dimensions={0}, use_global_device_ids=true | all-gather | bytes 557056 | tf_op jit(solution)/shard_map/all_gather | solution.py:112
  30.9 9.7 %all-gather = bf16[16,2,2,4096]{3,0,2,1:T(8,128)(2,1)S(1)} all-gather(bf16[8,2,2,4096]{3,0,2,1:T(8,128)(2,1)S(1)} %get-tuple-element.3), channel_id=2, replica_groups=mesh['grp'=2,'dev'=16] {'grp'}, dimensions={0}, use_global_device_ids=true | all-gather | bytes 786432 | tf_op jit(solution)/shard_map/all_gather | solution.py:117
  42.8 9.9 %fusion.25 = f32[4,128]{1,0:T(4,128)S(1)} fusion(f32[4,1,1,4096]{3,0,2,1:T(4,128)S(1)} %get-tuple-element.19, f32[4,1,1,4096]{3,0,2,1:T(4,128)S(1)} %get-tuple-element.18, f32[4096]{0:T(1024)S(1)} %get-tuple-element.38, f32[4096]{0:T(1024)S(1)} %get-tuple-element.39), kind=kOutput, calls=%fused_computation.58 | convolution fusion | flops 12124160 | bytes 165888 | tf_op jit(solution)/shard_map/dot_general | solution.py:45
  52.7 10.0 %convolution_add_fusion.6 = f32[4,128]{1,0:T(4,128)S(1)} fusion(f32[4,128]{1,0:T(4,128)S(1)} %fusion.25, f32[4,1,1,4096]{3,0,2,1:T(4,128)S(1)} %get-tuple-element.19, f32[4,1,1,4096]{3,0,2,1:T(4,128)S(1)} %get-tuple-element.18, f32[4096]{0:T(1024)S(1)} %get-tuple-element.38, f32[4096]{0:T(1024)S(1)} %get-tuple-element.39), kind=kOutput, calls=%fused_computation.54 | convolution fusion | flops 12648960 | bytes 167936 | tf_op jit(solution)/shard_map/dot_general | solution.py:46
  62.7 9.9 %fusion.24 = f32[4,128]{1,0:T(4,128)S(1)} fusion(f32[4,1,1,4096]{3,0,2,1:T(4,128)S(1)} %get-tuple-element.19, f32[4,1,1,4096]{3,0,2,1:T(4,128)S(1)} %get-tuple-element.18), kind=kOutput, calls=%fused_computation.57 | convolution fusion | flops 12124160 | bytes 133120 | tf_op jit(solution)/shard_map/dot_general | solution.py:45
  72.5 10.0 %convolution_add_fusion.5 = f32[4,128]{1,0:T(4,128)S(1)} fusion(f32[4,128]{1,0:T(4,128)S(1)} %fusion.24, f32[4,1,1,4096]{3,0,2,1:T(4,128)S(1)} %get-tuple-element.19, f32[4,1,1,4096]{3,0,2,1:T(4,128)S(1)} %get-tuple-element.18), kind=kOutput, calls=%fused_computation.53 | convolution fusion | flops 12648960 | bytes 135168 | tf_op jit(solution)/shard_map/dot_general | solution.py:46
  82.6 9.9 %fusion.23 = f32[4,128]{1,0:T(4,128)S(1)} fusion(f32[4,1,1,4096]{3,0,2,1:T(4,128)S(1)} %get-tuple-element.19, f32[4,1,1,4096]{3,0,2,1:T(4,128)S(1)} %get-tuple-element.18, f32[4096]{0:T(1024)S(1)} %get-tuple-element.36, f32[4096]{0:T(1024)S(1)} %get-tuple-element.37), kind=kOutput, calls=%fused_computation.56 | convolution fusion | flops 12124160 | bytes 165888 | tf_op jit(solution)/shard_map/dot_general | solution.py:45
  92.4 10.0 %convolution_add_fusion.4 = f32[4,128]{1,0:T(4,128)S(1)} fusion(f32[4,128]{1,0:T(4,128)S(1)} %fusion.23, f32[4,1,1,4096]{3,0,2,1:T(4,128)S(1)} %get-tuple-element.19, f32[4,1,1,4096]{3,0,2,1:T(4,128)S(1)} %get-tuple-element.18, f32[4096]{0:T(1024)S(1)} %get-tuple-element.36, f32[4096]{0:T(1024)S(1)} %get-tuple-element.37), kind=kOutput, calls=%fused_computation.52 | convolution fusion | flops 12648960 | bytes 167936 | tf_op jit(solution)/shard_map/dot_general | solution.py:46
  102.4 9.9 %fusion.26 = f32[4,128]{1,0:T(4,128)S(1)} fusion(f32[4,1,1,4096]{3,0,2,1:T(4,128)S(1)} %get-tuple-element.19, f32[4,1,1,4096]{3,0,2,1:T(4,128)S(1)} %get-tuple-element.18, f32[4096]{0:T(1024)S(1)} %get-tuple-element.40, f32[4096]{0:T(1024)S(1)} %get-tuple-element.41), kind=kOutput, calls=%fused_computation.59 | convolution fusion | flops 12124160 | bytes 165888 | tf_op jit(solution)/shard_map/dot_general | solution.py:45
  112.3 10.0 %convolution_add_fusion.7 = f32[4,128]{1,0:T(4,128)S(1)} fusion(f32[4,128]{1,0:T(4,128)S(1)} %fusion.26, f32[4,1,1,4096]{3,0,2,1:T(4,128)S(1)} %get-tuple-element.19, f32[4,1,1,4096]{3,0,2,1:T(4,128)S(1)} %get-tuple-element.18, f32[4096]{0:T(1024)S(1)} %get-tuple-element.40, f32[4096]{0:T(1024)S(1)} %get-tuple-element.41), kind=kOutput, calls=%fused_computation.55 | convolution fusion | flops 12648960 | bytes 167936 | tf_op jit(solution)/shard_map/dot_general | solution.py:46
  123.0 1.2 fusion.153
  124.8 1.0 add_add_fusion
  125.8 2.6 %fusion.7 = (bf16[128,4096]{1,0:T(8,128)(2,1)S(1)}, bf16[128,4096]{1,0:T(8,128)(2,1)S(1)}, bf16[128,4096]{1,0:T(8,128)(2,1)S(1)}, bf16[128,4096]{1,0:T(8,128)(2,...) fusion(f32[8,16,4096]{2,1,0:T(8,128)S(1)} %get-tuple-element.17, ...), kind=kLoop, calls=%fused_computation.20 | loop fusion | flops 16777216 | bytes 12681216 | tf_op jit(solution)/shard_map/convert_element_type | solution.py:43
  128.3 7.8 %fusion.30 = f32[128,128]{1,0:T(8,128)S(1)} fusion(bf16[128,4096]{1,0:T(8,128)(2,1)S(1)} %get-tuple-element.5), kind=kOutput, calls=%fused_computation.63 | convolution fusion | flops 142082048 | bytes 1114112 | tf_op jit(solution)/shard_map/dot_general | solution.py:45
  136.2 8.2 %convolution_add_fusion.3 = f32[128,128]{1,0:T(8,128)S(1)} fusion(f32[128,128]{1,0:T(8,128)S(1)} %fusion.30, bf16[128,4096]{1,0:T(8,128)(2,1)S(1)} %get-tuple-element.4), kind=kOutput, calls=%fused_computation.51 | convolution fusion | flops 142622720 | bytes 1179648 | tf_op jit(solution)/shard_map/dot_general | solution.py:46
  144.3 8.2 %fusion.29 = f32[128,128]{1,0:T(8,128)S(1)} fusion(bf16[128,4096]{1,0:T(8,128)(2,1)S(1)} %get-tuple-element.10), kind=kOutput, calls=%fused_computation.62 | convolution fusion | flops 142082048 | bytes 1114112 | tf_op jit(solution)/shard_map/dot_general | solution.py:45
  152.6 8.0 %convolution_add_fusion.2 = f32[128,128]{1,0:T(8,128)S(1)} fusion(f32[128,128]{1,0:T(8,128)S(1)} %fusion.29, bf16[128,4096]{1,0:T(8,128)(2,1)S(1)} %get-tuple-element.11), kind=kOutput, calls=%fused_computation.50 | convolution fusion | flops 142622720 | bytes 1179648 | tf_op jit(solution)/shard_map/dot_general | solution.py:46
  160.5 8.0 %fusion.28 = f32[128,128]{1,0:T(8,128)S(1)} fusion(bf16[128,4096]{1,0:T(8,128)(2,1)S(1)} %get-tuple-element.12), kind=kOutput, calls=%fused_computation.61 | convolution fusion | flops 142082048 | bytes 1114112 | tf_op jit(solution)/shard_map/dot_general | solution.py:45
  168.5 8.2 %convolution_add_fusion.1 = f32[128,128]{1,0:T(8,128)S(1)} fusion(f32[128,128]{1,0:T(8,128)S(1)} %fusion.28, bf16[128,4096]{1,0:T(8,128)(2,1)S(1)} %get-tuple-element.13), kind=kOutput, calls=%fused_computation.49 | convolution fusion | flops 142622720 | bytes 1179648 | tf_op jit(solution)/shard_map/dot_general | solution.py:46
  176.7 7.8 %fusion.27 = f32[128,128]{1,0:T(8,128)S(1)} fusion(bf16[128,4096]{1,0:T(8,128)(2,1)S(1)} %get-tuple-element.14), kind=kOutput, calls=%fused_computation.60 | convolution fusion | flops 142082048 | bytes 1114112 | tf_op jit(solution)/shard_map/dot_general | solution.py:45
  184.5 8.2 %convolution_add_fusion = f32[128,128]{1,0:T(8,128)S(1)} fusion(f32[128,128]{1,0:T(8,128)S(1)} %fusion.27, bf16[128,4096]{1,0:T(8,128)(2,1)S(1)} %get-tuple-element.15), kind=kOutput, calls=%fused_computation.48 | convolution fusion | flops 142622720 | bytes 1179648 | tf_op jit(solution)/shard_map/dot_general | solution.py:46
  (30 shorter events, 6.1 us)
Async XLA Ops:
  3.0 2.4 %copy-start = (f32[8,2,2,4096]{3,2,1,0:T(2,128)S(1)}, f32[8,2,2,4096]{3,2,1,0:T(2,128)}, u32[]{:S(2)}) copy-start(f32[8,2,2,4096]{3,2,1,0:T(2,128)} %param.5) | copy-start | bytes 1572868
  6.0 35.6 %copy-start.1 = (s32[1,1,2,2]{3,2,1,0:T(2,128)S(1)}, s32[1,1,2,2]{3,2,1,0:T(2,128)}, u32[]{:S(2)}) copy-start(s32[1,1,2,2]{3,2,1,0:T(2,128)} %param.7) | copy-start | bytes 52
where the time goes:
time: 196 us; the launch traced here: 194 us
  matrix products  145 us (74%)
  blocking collectives  34.3 us (17%)
  other arithmetic  6.76 us (3%)
  local copies, waits for them, and re-layouts  6.14 us (3%)
    dot_general x8, matrix products, cross_to_lags(): jnp.dot(rot_imag, sin_table, preferred_element_type=jnp.float32)  72.5 us
    dot_general x8, matrix products, cross_to_lags(): jnp.dot(rot_real, cos_table, preferred_element_type=jnp.float32)  71.3 us
    all_gather x1, blocking collectives, on_device(): group_corr = correlate(lax.all_gather(source, 'dev', axis=0, tiled=True))  24.6 us
    all_gather x1, blocking collectives, on_device(): gathered = lax.all_gather(white[None], 'grp', axis=0, tiled=True)  9.75 us

commit v1 on v0

--- a/solution.py
+++ b/solution.py
@@ -9,6 +9,34 @@
 LAG_BLK = 128
 BAND = 64
 source_block = 16
+
+
+def supply_all_array_all(load, axis_no):
+    load = jnp.moveaxis(load, 0, axis_no)
+    block_next = load.shape
+    return load.reshape(
+        *block_next[:axis_no],
+        block_next[axis_no] * block_next[axis_no + 1],
+        *block_next[axis_no + 2 :]
+    )
+
+
+def _rest_wall(mat, axis_tag):
+    out_arr = mat[None]
+    amount_of = lax.axis_size(axis_tag)
+    for tick in range(amount_of.bit_length() - 1):
+        d_next = 1 << tick
+        shaped = lax.ppermute(
+            out_arr, axis_tag, [(dev_j, dev_j ^ d_next) for dev_j in range(amount_of)]
+        )
+        e_now = jnp.stack([out_arr, shaped])
+        piece_now = lax.axis_index(axis_tag) >> tick & 1
+        out_arr = jnp.where(piece_now == 0, e_now, e_now[::-1]).reshape(-1, *mat.shape)
+    return out_arr
+
+
+def test_the_stocks(tile_in, sheet, dim_no):
+    return supply_all_array_all(_rest_wall(tile_in, sheet), dim_no)
 
 
 def whiten(spectra):
@@ -109,7 +137,7 @@
             return jnp.transpose(result, (1, 0, 2, 3)).reshape(channels_here, rows_here, LAGS)
         return outer_lags(white, shard_rows, tables)
 
-    group_corr = correlate(lax.all_gather(source, "dev", axis=0, tiled=True))
+    group_corr = correlate(test_the_stocks(source, "dev", 0))
     groups = lax.axis_size("grp")
     remote_ids = pair_remote.reshape(groups, -1)
     local_ids = pair_local.reshape(groups, -1)

time: 196 us -> 192 us (0.980)
  blocking collectives: 34.3 us -> 10.2 us
  waiting for transfers between devices: 0 us -> 10.4 us
  starting transfers between devices: 0 us -> 6.6 us
  other arithmetic: 6.76 us -> 8.93 us
    all_gather x1 -> x0, blocking collectives: 24.6 us -> none  [on_device(): group_corr = correlate(lax.all_gather(source, 'dev', axis=0, tiled=True))]
    ppermute x0 -> x4, waiting for transfers between devices: none -> 10.4 us  [_rest_wall(): lax.ppermute(out_arr, axis_tag, [(dev_j, dev_j ^ d_next) for dev_j in ran...]
    ppermute x0 -> x4, starting transfers between devices: none -> 6.6 us  [_rest_wall(): lax.ppermute(out_arr, axis_tag, [(dev_j, dev_j ^ d_next) for dev_j in ran...]
  transfers between devices with their start and end apart: 0 -> 4, of which waited for: 0 -> 1; matrix products, arithmetic and copies ran while one was open for 0% -> 44% of each run, Pallas kernels for 0% -> 0%
where the time goes in v1:
time: 192 us; the launch traced here: 189 us
  matrix products  145 us (76%)
  waiting for transfers between devices  10.4 us (5%)
  blocking collectives  10.2 us (5%)
  other arithmetic  8.93 us (5%)
  starting transfers between devices  6.6 us (3%)
  local copies, waits for them, and re-layouts  5.44 us (3%)
    dot_general x8, matrix products, cross_to_lags(): jnp.dot(rot_imag, sin_table, preferred_element_type=jnp.float32)  72.5 us
    dot_general x8, matrix products, cross_to_lags(): jnp.dot(rot_real, cos_table, preferred_element_type=jnp.float32)  71.9 us
    ppermute x4, waiting for transfers between devices, _rest_wall(): lax.ppermute(out_arr, axis_tag, [(dev_j, dev_j ^ d_next) for dev_j in ran...  10.4 us
    all_gather x1, blocking collectives, on_device(): gathered = lax.all_gather(white[None], 'grp', axis=0, tiled=True)  10.2 us
    ppermute x4, starting transfers between devices, _rest_wall(): lax.ppermute(out_arr, axis_tag, [(dev_j, dev_j ^ d_next) for dev_j in ran...  6.6 us
  transfers between devices with their start and end apart: 4, of which 1 were waited for; matrix products, arithmetic and copies ran while one was open for 44% of the time, Pallas kernels for 0%

profile of v1, /device:TPU:0, one launch (start us, length us, event | category | flops | bytes accessed | tf_op | source)
XLA Modules:
  0.0 188.7 jit_solution(4348212725715246316)
XLA Ops:
  1.3 1.4 copy.39
  5.0 10.2 %all-gather = bf16[16,2,2,4096]{3,0,2,1:T(8,128)(2,1)S(1)} all-gather(bf16[8,2,2,4096]{3,0,2,1:T(8,128)(2,1)S(1)} %get-tuple-element.3), channel_id=2, replica_groups=mesh['grp'=2,'dev'=16] {'grp'}, dimensions={0}, use_global_device_ids=true | all-gather | bytes 786432 | tf_op jit(solution)/shard_map/all_gather | solution.py:145
  17.7 10.4 %fusion.25 = f32[4,128]{1,0:T(4,128)S(1)} fusion(f32[4,1,1,4096]{3,0,2,1:T(4,128)S(1)} %get-tuple-element.23, f32[4,1,1,4096]{3,0,2,1:T(4,128)S(1)} %get-tuple-element.22, f32[4096]{0:T(1024)S(1)} %get-tuple-element.40, f32[4096]{0:T(1024)S(1)} %get-tuple-element.41), kind=kOutput, calls=%fused_computation.58 | convolution fusion | flops 12124160 | bytes 165888 | tf_op jit(solution)/shard_map/dot_general | solution.py:73
  28.1 10.0 %convolution_add_fusion.6 = f32[4,128]{1,0:T(4,128)S(1)} fusion(f32[4,128]{1,0:T(4,128)S(1)} %fusion.25, f32[4,1,1,4096]{3,0,2,1:T(4,128)S(1)} %get-tuple-element.23, f32[4,1,1,4096]{3,0,2,1:T(4,128)S(1)} %get-tuple-element.22, f32[4096]{0:T(1024)S(1)} %get-tuple-element.40, f32[4096]{0:T(1024)S(1)} %get-tuple-element.41), kind=kOutput, calls=%fused_computation.54 | convolution fusion | flops 12648960 | bytes 167936 | tf_op jit(solution)/shard_map/dot_general | solution.py:74
  38.1 9.9 %fusion.23 = f32[4,128]{1,0:T(4,128)S(1)} fusion(f32[4,1,1,4096]{3,0,2,1:T(4,128)S(1)} %get-tuple-element.23, f32[4,1,1,4096]{3,0,2,1:T(4,128)S(1)} %get-tuple-element.22, f32[4096]{0:T(1024)S(1)} %get-tuple-element.38, f32[4096]{0:T(1024)S(1)} %get-tuple-element.39), kind=kOutput, calls=%fused_computation.56 | convolution fusion | flops 12124160 | bytes 165888 | tf_op jit(solution)/shard_map/dot_general | solution.py:73
  48.0 10.0 %convolution_add_fusion.4 = f32[4,128]{1,0:T(4,128)S(1)} fusion(f32[4,128]{1,0:T(4,128)S(1)} %fusion.23, f32[4,1,1,4096]{3,0,2,1:T(4,128)S(1)} %get-tuple-element.23, f32[4,1,1,4096]{3,0,2,1:T(4,128)S(1)} %get-tuple-element.22, f32[4096]{0:T(1024)S(1)} %get-tuple-element.38, f32[4096]{0:T(1024)S(1)} %get-tuple-element.39), kind=kOutput, calls=%fused_computation.52 | convolution fusion | flops 12648960 | bytes 167936 | tf_op jit(solution)/shard_map/dot_general | solution.py:74
  58.0 9.9 %fusion.26 = f32[4,128]{1,0:T(4,128)S(1)} fusion(f32[4,1,1,4096]{3,0,2,1:T(4,128)S(1)} %get-tuple-element.23, f32[4,1,1,4096]{3,0,2,1:T(4,128)S(1)} %get-tuple-element.22, f32[4096]{0:T(1024)S(1)} %get-tuple-element.42, f32[4096]{0:T(1024)S(1)} %get-tuple-element.43), kind=kOutput, calls=%fused_computation.59 | convolution fusion | flops 12124160 | bytes 165888 | tf_op jit(solution)/shard_map/dot_general | solution.py:73
  67.9 10.0 %convolution_add_fusion.7 = f32[4,128]{1,0:T(4,128)S(1)} fusion(f32[4,128]{1,0:T(4,128)S(1)} %fusion.26, f32[4,1,1,4096]{3,0,2,1:T(4,128)S(1)} %get-tuple-element.23, f32[4,1,1,4096]{3,0,2,1:T(4,128)S(1)} %get-tuple-element.22, f32[4096]{0:T(1024)S(1)} %get-tuple-element.42, f32[4096]{0:T(1024)S(1)} %get-tuple-element.43), kind=kOutput, calls=%fused_computation.55 | convolution fusion | flops 12648960 | bytes 167936 | tf_op jit(solution)/shard_map/dot_general | solution.py:74
  78.1 1.8 collective-permute-start.1
  79.9 9.8 %fusion.24 = f32[4,128]{1,0:T(4,128)S(1)} fusion(f32[4,1,1,4096]{3,0,2,1:T(4,128)S(1)} %get-tuple-element.23, f32[4,1,1,4096]{3,0,2,1:T(4,128)S(1)} %get-tuple-element.22), kind=kOutput, calls=%fused_computation.57 | convolution fusion | flops 12124160 | bytes 133120 | tf_op jit(solution)/shard_map/dot_general | solution.py:73
  90.1 1.6 collective-permute-start.2
  91.7 10.0 %convolution_add_fusion.5 = f32[4,128]{1,0:T(4,128)S(1)} fusion(f32[4,128]{1,0:T(4,128)S(1)} %fusion.24, f32[4,1,1,4096]{3,0,2,1:T(4,128)S(1)} %get-tuple-element.23, f32[4,1,1,4096]{3,0,2,1:T(4,128)S(1)} %get-tuple-element.22), kind=kOutput, calls=%fused_computation.53 | convolution fusion | flops 12648960 | bytes 135168 | tf_op jit(solution)/shard_map/dot_general | solution.py:74
  102.3 2.7 %collective-permute-start.3 = (bf16[8,1,2,2,4096]{4,3,2,0,1:T(2,128)(2,1)S(1)}, bf16[8,1,2,2,4096]{4,3,2,0,1:T(2,128)(2,1)S(1)}, u32[]{:S(2)}, u32[]{:S(2)}) collective-permute-start(bf16[8,1,2,2,4096]{4,3,2,0,1:T(2,128)(2,1)S(1)} %bitcast.220), channel_id=1, source_target_pairs={{0,8},{1,9},{2,10},{3,11},{4,12},{5,13},{6,14},{7,15},{8,0},{9,1},... | collective-permute-start | bytes 786440 | tf_op jit(solution)/shard_map/ppermute | solution.py:29
  105.7 10.4 %collective-permute-done.3 = bf16[8,1,2,2,4096]{4,3,2,0,1:T(2,128)(2,1)S(1)} collective-permute-done((bf16[8,1,2,2,4096]{4,3,2,0,1:T(2,128)(2,1)S(1)}, bf16[8,1,2,2,4096]{4,3,2,0,1:T(2,128)(2,1)S(1)}, u32[]{:S(2)}, u32[]{:S(2)}) %collective-permute-start.3) | collective-permute-done | bytes 262176 | tf_op jit(solution)/shard_map/ppermute | solution.py:29
  117.9 1.1 fusion.155
  120.7 2.6 %fusion.7 = (bf16[128,4096]{1,0:T(8,128)(2,1)S(1)}, bf16[128,4096]{1,0:T(8,128)(2,1)S(1)}, bf16[128,4096]{1,0:T(8,128)(2,1)S(1)}, bf16[128,4096]{1,0:T(8,128)(2,...) fusion(f32[8,16,4096]{2,1,0:T(8,128)S(1)} %get-tuple-element.17, ...), kind=kLoop, calls=%fused_computation.20 | loop fusion | flops 16777216 | bytes 12681216 | tf_op jit(solution)/shard_map/convert_element_type | solution.py:71
  123.2 7.8 %fusion.30 = f32[128,128]{1,0:T(8,128)S(1)} fusion(bf16[128,4096]{1,0:T(8,128)(2,1)S(1)} %get-tuple-element.5), kind=kOutput, calls=%fused_computation.63 | convolution fusion | flops 142082048 | bytes 1114112 | tf_op jit(solution)/shard_map/dot_general | solution.py:73
  131.1 8.0 %fusion.29 = f32[128,128]{1,0:T(8,128)S(1)} fusion(bf16[128,4096]{1,0:T(8,128)(2,1)S(1)} %get-tuple-element.10), kind=kOutput, calls=%fused_computation.62 | convolution fusion | flops 142082048 | bytes 1114112 | tf_op jit(solution)/shard_map/dot_general | solution.py:73
  139.1 8.2 %fusion.28 = f32[128,128]{1,0:T(8,128)S(1)} fusion(bf16[128,4096]{1,0:T(8,128)(2,1)S(1)} %get-tuple-element.12), kind=kOutput, calls=%fused_computation.61 | convolution fusion | flops 142082048 | bytes 1114112 | tf_op jit(solution)/shard_map/dot_general | solution.py:73
  147.3 7.8 %fusion.27 = f32[128,128]{1,0:T(8,128)S(1)} fusion(bf16[128,4096]{1,0:T(8,128)(2,1)S(1)} %get-tuple-element.14), kind=kOutput, calls=%fused_computation.60 | convolution fusion | flops 142082048 | bytes 1114112 | tf_op jit(solution)/shard_map/dot_general | solution.py:73
  155.2 8.1 %convolution_add_fusion.3 = f32[128,128]{1,0:T(8,128)S(1)} fusion(f32[128,128]{1,0:T(8,128)S(1)} %fusion.30, bf16[128,4096]{1,0:T(8,128)(2,1)S(1)} %get-tuple-element.4), kind=kOutput, calls=%fused_computation.51 | convolution fusion | flops 142622720 | bytes 1179648 | tf_op jit(solution)/shard_map/dot_general | solution.py:74
  163.3 8.2 %convolution_add_fusion.2 = f32[128,128]{1,0:T(8,128)S(1)} fusion(f32[128,128]{1,0:T(8,128)S(1)} %fusion.29, bf16[128,4096]{1,0:T(8,128)(2,1)S(1)} %get-tuple-element.11), kind=kOutput, calls=%fused_computation.50 | convolution fusion | flops 142622720 | bytes 1179648 | tf_op jit(solution)/shard_map/dot_general | solution.py:74
  171.5 8.0 %convolution_add_fusion.1 = f32[128,128]{1,0:T(8,128)S(1)} fusion(f32[128,128]{1,0:T(8,128)S(1)} %fusion.28, bf16[128,4096]{1,0:T(8,128)(2,1)S(1)} %get-tuple-element.13), kind=kOutput, calls=%fused_computation.49 | convolution fusion | flops 142622720 | bytes 1179648 | tf_op jit(solution)/shard_map/dot_general | solution.py:74
  179.4 8.2 %convolution_add_fusion = f32[128,128]{1,0:T(8,128)S(1)} fusion(f32[128,128]{1,0:T(8,128)S(1)} %fusion.27, bf16[128,4096]{1,0:T(8,128)(2,1)S(1)} %get-tuple-element.15), kind=kOutput, calls=%fused_computation.48 | convolution fusion | flops 142622720 | bytes 1179648 | tf_op jit(solution)/shard_map/dot_general | solution.py:74
  (51 shorter events, 10.6 us)
Async XLA Ops:
  1.3 2.4 %copy-start = (f32[8,2,2,4096]{3,2,1,0:T(2,128)S(1)}, f32[8,2,2,4096]{3,2,1,0:T(2,128)}, u32[]{:S(2)}) copy-start(f32[8,2,2,4096]{3,2,1,0:T(2,128)} %param.5) | copy-start | bytes 1572868
  3.2 11.9 %copy-start.2 = (s32[1,1,2,2]{3,2,1,0:T(2,128)S(1)}, s32[1,1,2,2]{3,2,1,0:T(2,128)}, u32[]{:S(2)}) copy-start(s32[1,1,2,2]{3,2,1,0:T(2,128)} %param.8) | copy-start | bytes 52
  4.2 73.7 %collective-permute-start = (bf16[1,1,2,2,4096]{4,3,2,1,0:T(2,128)(2,1)S(1)}, bf16[1,1,2,2,4096]{4,3,2,1,0:T(2,128)(2,1)S(1)}, u32[]{:S(2)}, u32[]{:S(2)}) collective-permute-start(bf16[1,1,2,2,4096]{4,3,2,1,0:T(2,128)(2,1)S(1)} %broadcast_in_dim_reshape.2), channel_id=1, source_target_pairs={{0,1},{1,0},{2,3},{3,2},{4,5},{5,4},{6,7},{7,6},{8,9},{9,8},{10,11... | collective-permute-start | bytes 98312 | tf_op jit(solution)/shard_map/ppermute | solution.py:29
  15.2 1.4 copy-start.1
  78.1 11.6 %collective-permute-start.1 = (bf16[2,1,2,2,4096]{4,3,2,0,1:T(2,128)(2,1)S(1)}, bf16[2,1,2,2,4096]{4,3,2,0,1:T(2,128)(2,1)S(1)}, u32[]{:S(2)}, u32[]{:S(2)}) collective-permute-start(bf16[2,1,2,2,4096]{4,3,2,0,1:T(2,128)(2,1)S(1)} %get-tuple-element.33), channel_id=1, source_target_pairs={{0,2},{1,3},{2,0},{3,1},{4,6},{5,7},{6,4},{7,5},{8,10},{9,11},{10,... | collective-permute-start | bytes 196616 | tf_op jit(solution)/shard_map/ppermute | solution.py:29
  90.0 14.9 %copy-start.3 = (s32[1,1,2]{2,1,0:T(1,128)S(1)}, s32[1,1,2]{2,1,0:T(1,128)}, u32[]{:S(2)}) copy-start(s32[1,1,2]{2,1,0:T(1,128)} %param.9) | copy-start | bytes 28
  90.1 11.6 %collective-permute-start.2 = (bf16[4,1,2,2,4096]{4,3,2,0,1:T(2,128)(2,1)S(1)}, bf16[4,1,2,2,4096]{4,3,2,0,1:T(2,128)(2,1)S(1)}, u32[]{:S(2)}, u32[]{:S(2)}) collective-permute-start(bf16[4,1,2,2,4096]{4,3,2,0,1:T(2,128)(2,1)S(1)} %bitcast.223), channel_id=1, source_target_pairs={{0,4},{1,5},{2,6},{3,7},{4,0},{5,1},{6,2},{7,3},{8,12},{9,13},{10,... | collective-permute-start | bytes 393224 | tf_op jit(solution)/shard_map/ppermute | solution.py:29
  102.3 13.8 %collective-permute-start.3 = (bf16[8,1,2,2,4096]{4,3,2,0,1:T(2,128)(2,1)S(1)}, bf16[8,1,2,2,4096]{4,3,2,0,1:T(2,128)(2,1)S(1)}, u32[]{:S(2)}, u32[]{:S(2)}) collective-permute-start(bf16[8,1,2,2,4096]{4,3,2,0,1:T(2,128)(2,1)S(1)} %bitcast.220), channel_id=1, source_target_pairs={{0,8},{1,9},{2,10},{3,11},{4,12},{5,13},{6,14},{7,15},{8,0},{9,1},... | collective-permute-start | bytes 786440 | tf_op jit(solution)/shard_map/ppermute | solution.py:29
